TPU v7x, 128 devices: a whole 4x4x4 slice. The times are simulated.
128 devices in a mesh: tm: 8 (over y_lo, x), space: 16 (over y_hi, z, core).
Axes of the slice: x: 4, y: 4 (y_hi: 2, y_lo: 2; y = y_hi * 2 + y_lo), z: 4, core: 2. Of those that a mesh axis runs over, the one named last changes fastest.
Arguments:
- frames_in: bfloat16 [32, 64, 64, 512], P('tm', 'space'), may hold values from -6 to 6
- spatial_kernel: bfloat16 [3, 3, 512, 512], replicated, may hold values from -0.09375 to 0.09375
- temporal_kernel: bfloat16 [3, 512, 512], replicated, may hold values from -0.15625 to 0.15625
- norm_gain: float32 [512], replicated, may hold values from 0.1 to 1.9
- query_weight: bfloat16 [512, 512], replicated, may hold values from -2 to 2
- key_weight: bfloat16 [512, 512], replicated, may hold values from -2 to 2
- value_weight: bfloat16 [512, 512], replicated, may hold values from -0.25 to 0.25
- out_weight: bfloat16 [512, 512], replicated, may hold values from -0.25 to 0.25
- cotangent: bfloat16 [32, 64, 64, 512], P('tm', 'space'), may hold values from -6 to 6
Outputs:
- encoded: bfloat16 [32, 64, 64, 512], P('tm', 'space')
- kernel_grad: float32 [3, 512, 512], P(None, 'tm', 'space')
All inputs are finite; a program needn't handle non-finite values.
Results may differ from a plain program's by a relative error of at most 0.007.
Values may be sent and summed in bfloat16 or wider, within the bound.
A program may use at most 128 MiB of HBM per device.

v0:
```python
import jax
import jax.numpy as jnp
from jax import lax
from jax.sharding import PartitionSpec as P


def extended_2(cells, sides, width):
    for axis, dim in sides:
        count = lax.axis_size(axis)
        ends = count - 1
        head = lax.slice_in_dim(cells, 0, width, axis=dim)
        tail = lax.slice_in_dim(cells, cells.shape[dim] - width, cells.shape[dim], axis=dim)
        cells = jnp.concatenate(
            [
                lax.ppermute(tail, axis, [(i, (i + 1) % count) for i in range(ends)]),
                cells,
                lax.ppermute(head, axis, [((i + 1) % count, i) for i in range(ends)]),
            ],
            axis=dim,
        )
    return cells


def from_behind(value, axis, steps):
    count = lax.axis_size(axis)
    first, last = (max(0, -steps), min(count, count - steps))
    return lax.ppermute(value, axis, [(source, source + steps) for source in range(first, last)])


def project_all(normed, query_weight, key_weight, value_weight, lead, positions, chans):
    query = (
        jnp.dot(normed, query_weight, preferred_element_type=jnp.float32)
        .astype(jnp.bfloat16)
        .reshape(lead, positions, chans)
    )
    key = (
        jnp.dot(normed, key_weight, preferred_element_type=jnp.float32)
        .astype(jnp.bfloat16)
        .reshape(lead, positions, chans)
    )
    value = (
        jnp.dot(normed, value_weight, preferred_element_type=jnp.float32)
        .astype(jnp.bfloat16)
        .reshape(lead, positions, chans)
    )
    return (query, key, value)


def on_device(
    frames_in,
    spatial_kernel,
    temporal_kernel,
    norm_gain,
    query_weight,
    key_weight,
    value_weight,
    out_weight,
    cotangent,
):
    frames, rows, cols, chans = frames_in.shape
    padded = extended_2(frames_in, (("space", 1),), 1)
    padded = jnp.pad(padded, ((0, 0), (0, 0), (1, 1), (0, 0)))
    spatial = jnp.zeros((frames * rows * cols, chans), jnp.float32)
    for di in range(3):
        for dj in range(3):
            piece = padded[:, di : di + rows, dj : dj + cols, :].reshape(-1, chans)
            spatial = spatial + jnp.dot(
                piece, spatial_kernel[di, dj], preferred_element_type=jnp.float32
            )
    act = jax.nn.silu(spatial).astype(jnp.bfloat16).reshape(frames, rows, cols, chans)
    earlier = from_behind(act[frames - 2 :], "tm", 1)
    extended = jnp.concatenate([earlier, act], axis=0)
    temporal = jnp.zeros((frames * rows * cols, chans), jnp.float32)
    flat_grad = cotangent.reshape(-1, chans)
    grads = []
    for tap in range(3):
        shifted = extended[2 - tap : 2 - tap + frames].reshape(-1, chans)
        temporal = temporal + jnp.dot(
            shifted, temporal_kernel[tap], preferred_element_type=jnp.float32
        )
        grads.append(
            jnp.einsum("nc,nd->cd", shifted, flat_grad, preferred_element_type=jnp.float32)
        )
    partial_grad = jnp.stack(grads, axis=0)
    hidden = (frames_in.reshape(-1, chans).astype(jnp.float32) + temporal).astype(jnp.bfloat16)
    wide = hidden.astype(jnp.float32)
    normed = (
        wide / jnp.sqrt(jnp.mean(wide * wide, axis=1, keepdims=True) + 1e-06) * norm_gain
    ).astype(jnp.bfloat16)
    positions = rows * cols
    query, key, value = project_all(
        normed, query_weight, key_weight, value_weight, frames, positions, chans
    )
    first_frame = lax.axis_index("tm") * frames
    query_frames = first_frame + jnp.arange(frames)
    scale = 1.0 / jnp.sqrt(jnp.float32(chans))
    running_max = jnp.full((frames, positions), -1e30, jnp.float32)
    key_piece = lax.all_gather(key, "tm", axis=0, tiled=True)
    value_piece = lax.all_gather(value, "tm", axis=0, tiled=True)
    scores = (
        jnp.einsum("anc,bnc->abn", query, key_piece, preferred_element_type=jnp.float32) * scale
    )
    key_frames = jnp.arange(key_piece.shape[0])
    allowed = (key_frames[None, :] <= query_frames[:, None])[:, :, None]
    masked = jnp.where(allowed, scores, jnp.float32(-1e30))
    new_max = jnp.maximum(running_max, jnp.max(masked, axis=1))
    expon = jnp.where(allowed, jnp.exp(scores - new_max[:, None, :]), jnp.float32(0.0))
    new_sum = jnp.sum(expon, axis=1)
    new_acc = jnp.einsum("abn,bnc->anc", expon, value_piece.astype(jnp.float32))
    attended = (new_acc / new_sum[:, :, None]).astype(jnp.bfloat16)
    encoded = (
        wide + jnp.dot(attended.reshape(-1, chans), out_weight, preferred_element_type=jnp.float32)
    ).astype(jnp.bfloat16)
    section = lax.psum_scatter(partial_grad, "space", scatter_dimension=2, tiled=True)
    kernel_grad = lax.psum_scatter(section, "tm", scatter_dimension=1, tiled=True)
    return (encoded.reshape(frames, rows, cols, chans), kernel_grad)


def solution(mesh):
    in_specs = (
        P("tm", "space", None, None),
        P(),
        P(),
        P(),
        P(),
        P(),
        P(),
        P(),
        P("tm", "space", None, None),
    )
    out_specs = (P("tm", "space", None, None), P(None, "tm", "space"))
    return jax.shard_map(
        on_device, mesh=mesh, in_specs=in_specs, out_specs=out_specs, check_vma=False
    )
```

profile of v0, /device:TPU:1, one launch (start us, length us, event | category | flops | bytes accessed | tf_op | source)
XLA Modules:
  0.0 465.0 jit_solution(18101736379835137255)
XLA Ops:
  7.2 1.1 fusion.74
  8.4 5.1 %collective-permute-start = (bf16[4,1,64,512]{3,2,1,0:T(8,128)(2,1)S(1)}, bf16[4,1,64,512]{3,2,1,0:T(8,128)(2,1)S(1)}, u32[]{:S(2)}, u32[]{:S(2)}) collective-permute-start(bf16[4,1,64,512]{3,2,1,0:T(8,128)(2,1)S(1)} %get-tuple-element.20), channel_id=1, source_target_pairs={{0,1},{1,2},{2,3},{3,4},{4,5},{5,6},{6,7},{7,8},{8,9},{9,10},{10,1... | collective-permute-start | bytes 786440 | tf_op jit(solution)/shard_map/ppermute | solution.py:15
  13.5 1.9 collective-permute-start.1
  15.4 2.1 fusion.41
  17.5 3.7 collective-permute-done.1
  21.2 0.9 fusion.14
  22.1 1.3 fusion.73
  28.8 1.6 multiply_convert_fusion
  30.5 3.1 collective-permute-start.2
  33.6 0.7 convolution_bitcast_fusion
  34.3 7.2 %collective-permute-done.2 = bf16[2,4,64,512]{3,2,1,0:T(8,128)(2,1)S(1)} collective-permute-done((bf16[2,4,64,512]{3,2,1,0:T(8,128)(2,1)S(1)}, bf16[2,4,64,512]{3,2,1,0:T(8,128)(2,1)S(1)}, u32[]{:S(2)}, u32[]{:S(2)}) %collective-permute-start.2) | collective-permute-done | bytes 524320 | tf_op jit(solution)/shard_map/ppermute | solution.py:27
  43.0 2.0 pad_maximum_fusion
  45.0 5.1 %copy.30 = f32[3,512,512]{1,0,2:T(4,128)} copy(f32[3,512,512]{2,1,0:T(8,128)} %pad_maximum_fusion) | data formatting | bytes 6291456 | tf_op jit(solution)/shard_map/stack | solution.py:84
  52.0 1.7 fusion.29
  53.8 1.4 fusion.24
  56.1 1.0 fusion.5
  57.1 148.1 %all-reduce.4.cloned.1.call-done = f32[3,512,512]{1,0,2:T(4,128)} async-done(((f32[3,512,512]{1,0,2:T(4,128)}), f32[3,512,512]{1,0,2:T(4,128)}) %all-reduce.4.cloned.1.call-update) | async-done | bytes 3145744
  205.3 1.0 constant_dynamic-slice_fusion
  206.3 7.6 %copy.34 = f32[3,512,32]{0,2,1:T(8,128)} copy(f32[3,512,32]{1,0,2:T(4,128)S(1)} %constant_dynamic-slice_fusion) | data formatting | bytes 393216
  213.9 8.8 %reshape.117 = f32[512,96]{1,0:T(8,128)} reshape(f32[512,32,3]{2,1,0:T(8,128)} %bitcast.105) | data formatting | bytes 393216
  222.8 1.8 convolution_convert_fusion.1
  224.9 1.7 convolution_convert_fusion.2
  226.8 1.7 convolution_convert_fusion
  228.5 27.6 %reduce-scatter.4.cloned.1.call-done = f32[64,96]{1,0:T(8,128)} async-done(((f32[512,96]{1,0:T(8,128)}), f32[64,96]{1,0:T(8,128)}) %reduce-scatter.4.cloned.1.call-update) | async-done | bytes 24592
  256.0 1.8 reshape.118
  257.9 1.2 copy.31
  259.1 94.7 %all-gather.5.cloned.1.call-done = bf16[32,256,512]{2,1,0:T(8,128)(2,1)} async-done(((bf16[4,256,512]{2,1,0:T(8,128)(2,1)}), bf16[32,256,512]{2,1,0:T(8,128)(2,1)}) %all-gather.5.cloned.1.call-update) | async-done | bytes 8388624 | tf_op jit(solution)/shard_map/all_gather | solution.py:98
  353.8 9.0 %select_reduce_fusion = (f32[4,256]{0,1:T(8,128)S(1)}, f32[4,32,256]{1,0,2:T(4,128)S(1)}) fusion(pred[4,32]{1,0:T(4,128)(4,1)S(1)} %iota_compare_fusion.2, bf16[4,256,512]{2,1,0:T(8,128)(2,1)} %bitcast.128, bf16[32,256,512]{2,1,0:T(8,128)(2,1)} %all-gather.5.cloned.1.call-done), kind=kOutput, calls=%fused_computation.66 | convolution fusion | flops 33651712 | bytes 9572480 | tf_op jit(solution)/shard_map/anc,bnc->abn/dot_general | solution.py:101
  363.5 83.2 %all-gather.3.cloned.1.call-done = bf16[32,256,512]{2,1,0:T(8,128)(2,1)} async-done(((bf16[4,256,512]{2,1,0:T(8,128)(2,1)}), bf16[32,256,512]{2,1,0:T(8,128)(2,1)}) %all-gather.3.cloned.1.call-update) | async-done | bytes 8388624 | tf_op jit(solution)/shard_map/all_gather | solution.py:99
  446.7 9.0 %fusion.9 = bf16[4,256,512]{2,0,1:T(4,128)(2,1)S(1)} fusion(bf16[32,256,512]{2,1,0:T(8,128)(2,1)} %all-gather.3.cloned.1.call-done, f32[4,256]{0,1:T(8,128)S(1)} %fusion.63, f32[4,32,256]{1,0,2:T(4,128)S(1)} %get-tuple-element.25, f32[4,256]{0,1:T(8,128)S(1)} %broadcast_maximum_fusion, pred[4,32]{1,0:T(4,128)(4,1)S(1)} %iota_compare_fusion.2), kind=kOutput, calls=%fused_computation.21 | convolution fusion | flops 34668544 | bytes 9576576 | tf_op jit(solution)/shard_map/abn,bnc->anc/dot_general | solution.py:109
  455.9 0.8 copy-done.8
  456.7 1.7 fusion.8
  (54 shorter events, 10.4 us)
Async XLA Ops:
  7.2 26.4 %copy-start = (bf16[4,4,64,512]{3,2,1,0:T(8,128)(2,1)S(1)}, bf16[4,4,64,512]{3,2,1,0:T(8,128)(2,1)}, u32[]{:S(2)}) copy-start(bf16[4,4,64,512]{3,2,1,0:T(8,128)(2,1)} %param.17) | copy-start | bytes 3145732
  7.2 198.1 %all-reduce.4.cloned.1.call-start = ((), (), s32[]{:S(2)}) async-start(), calls=%async_computation.4 | async-start | bytes 8388608
  8.4 12.8 %copy-start.2 = (bf16[4,4,64,512]{3,2,1,0:T(8,128)(2,1)S(1)}, bf16[4,4,64,512]{3,2,1,0:T(8,128)(2,1)}, u32[]{:S(2)}) copy-start(bf16[4,4,64,512]{3,2,1,0:T(8,128)(2,1)} %param.9) | copy-start | bytes 3145732
  8.4 9.1 %collective-permute-start = (bf16[4,1,64,512]{3,2,1,0:T(8,128)(2,1)S(1)}, bf16[4,1,64,512]{3,2,1,0:T(8,128)(2,1)S(1)}, u32[]{:S(2)}, u32[]{:S(2)}) collective-permute-start(bf16[4,1,64,512]{3,2,1,0:T(8,128)(2,1)S(1)} %get-tuple-element.20), channel_id=1, source_target_pairs={{0,1},{1,2},{2,3},{3,4},{4,5},{5,6},{6,7},{7,8},{8,9},{9,10},{10,1... | collective-permute-start | bytes 786440 | tf_op jit(solution)/shard_map/ppermute | solution.py:15
  13.5 7.7 %collective-permute-start.1 = (bf16[4,1,64,512]{3,2,1,0:T(8,128)(2,1)S(1)}, bf16[4,1,64,512]{3,2,1,0:T(8,128)(2,1)S(1)}, u32[]{:S(2)}, u32[]{:S(2)}) collective-permute-start(bf16[4,1,64,512]{3,2,1,0:T(8,128)(2,1)S(1)} %get-tuple-element.21), channel_id=1, source_target_pairs={{1,0},{2,1},{3,2},{4,3},{5,4},{6,5},{7,6},{8,7},{9,8},{10,9},{11,1... | collective-permute-start | bytes 786440 | tf_op jit(solution)/shard_map/ppermute | solution.py:17
  21.2 2.3 slice-start
  22.1 1.6 slice-start.1
  30.5 11.0 %collective-permute-start.2 = (bf16[2,4,64,512]{3,2,1,0:T(8,128)(2,1)S(1)}, bf16[2,4,64,512]{3,2,1,0:T(8,128)(2,1)S(1)}, u32[]{:S(2)}, u32[]{:S(2)}) collective-permute-start(bf16[2,4,64,512]{3,2,1,0:T(8,128)(2,1)S(1)} %bitcast.127), channel_id=1, source_target_pairs={{0,16},{16,32},{32,48},{48,64},{64,80},{80,96},{96,112},{1,17},{17... | collective-permute-start | bytes 1572872 | tf_op jit(solution)/shard_map/ppermute | solution.py:27
  41.5 0.8 copy-start.4
  50.1 0.7 copy-start.10
  50.2 205.9 %reduce-scatter.4.cloned.1.call-start = ((), (), s32[]{:S(2)}) async-start(), calls=%async_computation.3 | async-start | bytes 294912
  53.8 1.6 copy-start.3
  213.9 8.9 %copy-start.5 = (bf16[512,512]{1,0:T(8,128)(2,1)S(1)}, bf16[512,512]{1,0:T(8,128)(2,1)}, u32[]{:S(2)}) copy-start(bf16[512,512]{1,0:T(8,128)(2,1)} %param.14) | copy-start | bytes 1572868
  213.9 8.9 %copy-start.9 = (f32[512]{0:T(512)S(1)}, f32[512]{0:T(512)}, u32[]{:S(2)}) copy-start(f32[512]{0:T(512)} %param.12) | copy-start | bytes 6148
  222.7 131.1 %all-gather.5.cloned.1.call-start = ((), (), s32[]{:S(2)}) async-start(), calls=%async_computation.2 | async-start | bytes 9437184 | tf_op jit(solution)/shard_map/all_gather | solution.py:98
  222.8 2.1 copy-start.6
  224.6 2.2 copy-start.7
  224.6 222.1 %all-gather.3.cloned.1.call-start = ((), (), s32[]{:S(2)}) async-start(), calls=%async_computation.1 | async-start | bytes 9437184 | tf_op jit(solution)/shard_map/all_gather | solution.py:99
  455.7 1.0 copy-start.8
  455.7 2.7 copy-start.1
Sparse Core Ops, SparseCore 0:
  50.3 154.9 all-reduce.3
  222.8 33.1 reduce-scatter.3
  257.8 95.9 all-gather.4
  356.0 90.6 all-gather.2
where the time goes:
time: 466 us; the launch traced here: 465 us
  waiting for transfers between devices  364 us (78%)
  matrix products  39.1 us (8%)
  local copies, waits for them, and re-layouts  30.6 us (7%)
  between operations  14.7 us (3%)
  starting transfers between devices  10.7 us (2%)
  other arithmetic  5.3 us (1%)
    unnamed x6, waiting for transfers between devices  176 us
    all_gather x1, waiting for transfers between devices, on_device(): key_piece = lax.all_gather(key, 'tm', axis=0, tiled=True)  94.7 us
    all_gather x1, waiting for transfers between devices, on_device(): value_piece = lax.all_gather(value, 'tm', axis=0, tiled=True)  83.2 us
    unnamed x32, local copies, waits for them, and re-layouts  22.8 us
  transfers between devices with their start and end apart: 7, of which 6 were waited for; matrix products, arithmetic and copies ran while one was open for 6% of the time, Pallas kernels for 0%

commit v1 on v0

--- a/solution.py
+++ b/solution.py
@@ -95,7 +95,8 @@
     query_frames = first_frame + jnp.arange(frames)
     scale = 1.0 / jnp.sqrt(jnp.float32(chans))
     running_max = jnp.full((frames, positions), -1e30, jnp.float32)
-    key_piece = lax.all_gather(key, "tm", axis=0, tiled=True)
+    sent = jnp.stack([key] * lax.axis_size("tm"))
+    key_piece = jnp.concatenate(lax.all_to_all(sent, "tm", 0, 0), axis=0)
     value_piece = lax.all_gather(value, "tm", axis=0, tiled=True)
     scores = (
         jnp.einsum("anc,bnc->abn", query, key_piece, preferred_element_type=jnp.float32) * scale

time: 466 us -> 480 us (1.030)
  local copies, waits for them, and re-layouts: 30.6 us -> 58 us
  waiting for transfers between devices: 364 us -> 350 us
  starting transfers between devices: 10.7 us -> 15.8 us
    all_gather x1 -> x0, waiting for transfers between devices: 94.7 us -> none  [on_device(): key_piece = lax.all_gather(key, 'tm', axis=0, tiled=True)]
    unnamed x6 -> x5, waiting for transfers between devices: 176 us -> 223 us
    all_to_all x0 -> x1, waiting for transfers between devices: none -> 27.3 us  [on_device(): key_piece = jnp.concatenate(lax.all_to_all(sent, 'tm', 0, 0), axis=0)]
    reshape x0 -> x1, local copies, waits for them, and re-layouts: none -> 12.5 us  [on_device(): key_piece = jnp.concatenate(lax.all_to_all(sent, 'tm', 0, 0), axis=0)]
    all_to_all x0 -> x1, local copies, waits for them, and re-layouts: none -> 8.58 us  [on_device(): key_piece = jnp.concatenate(lax.all_to_all(sent, 'tm', 0, 0), axis=0)]
    another operation x0 -> x2, local copies, waits for them, and re-layouts: none -> 6.2 us  [on_device(): sent = jnp.stack([key] * lax.axis_size('tm'))]
    all_gather x1, waiting for transfers between devices: 83.2 us -> 88.8 us  [on_device(): value_piece = lax.all_gather(value, 'tm', axis=0, tiled=True)]
    all_to_all x0 -> x1, starting transfers between devices: none -> 5.4 us  [on_device(): key_piece = jnp.concatenate(lax.all_to_all(sent, 'tm', 0, 0), axis=0)]
  transfers between devices with their start and end apart: 7 -> 7, of which waited for: 6 -> 6; matrix products, arithmetic and copies ran while one was open for 6% -> 10% of each run, Pallas kernels for 0% -> 0%
where the time goes in v1:
time: 480 us; the launch traced here: 479 us
  waiting for transfers between devices  350 us (73%)
  local copies, waits for them, and re-layouts  58 us (12%)
  matrix products  35.3 us (7%)
  starting transfers between devices  15.8 us (3%)
  between operations  14.7 us (3%)
  other arithmetic  5.29 us (1%)
    unnamed x5, waiting for transfers between devices  223 us
    all_gather x1, waiting for transfers between devices, on_device(): value_piece = lax.all_gather(value, 'tm', axis=0, tiled=True)  88.8 us
    all_to_all x1, waiting for transfers between devices, on_device(): key_piece = jnp.concatenate(lax.all_to_all(sent, 'tm', 0, 0), axis=0)  27.3 us
    unnamed x32, local copies, waits for them, and re-layouts  22.8 us
    reshape x1, local copies, waits for them, and re-layouts, on_device(): key_piece = jnp.concatenate(lax.all_to_all(sent, 'tm', 0, 0), axis=0)  12.5 us
  transfers between devices with their start and end apart: 7, of which 6 were waited for; matrix products, arithmetic and copies ran while one was open for 10% of the time, Pallas kernels for 0%

profile of v1, /device:TPU:1, one launch (start us, length us, event | category | flops | bytes accessed | tf_op | source)
XLA Modules:
  0.0 479.4 jit_solution(9625312876288435312)
XLA Ops:
  7.2 1.1 fusion.67
  8.4 5.1 %collective-permute-start = (bf16[4,1,64,512]{3,2,1,0:T(8,128)(2,1)S(1)}, bf16[4,1,64,512]{3,2,1,0:T(8,128)(2,1)S(1)}, u32[]{:S(2)}, u32[]{:S(2)}) collective-permute-start(bf16[4,1,64,512]{3,2,1,0:T(8,128)(2,1)S(1)} %get-tuple-element.20), channel_id=1, source_target_pairs={{0,1},{1,2},{2,3},{3,4},{4,5},{5,6},{6,7},{7,8},{8,9},{9,10},{10,1... | collective-permute-start | bytes 786440 | tf_op jit(solution)/shard_map/ppermute | solution.py:15
  13.5 1.9 collective-permute-start.1
  15.4 2.1 fusion.34
  17.5 3.7 collective-permute-done.1
  22.1 1.3 fusion.66
  28.8 1.6 multiply_convert_fusion
  30.5 3.1 collective-permute-start.2
  34.4 7.2 %collective-permute-done.2 = bf16[2,4,64,512]{3,2,1,0:T(8,128)(2,1)S(1)} collective-permute-done((bf16[2,4,64,512]{3,2,1,0:T(8,128)(2,1)S(1)}, bf16[2,4,64,512]{3,2,1,0:T(8,128)(2,1)S(1)}, u32[]{:S(2)}, u32[]{:S(2)}) %collective-permute-start.2) | collective-permute-done | bytes 524320 | tf_op jit(solution)/shard_map/ppermute | solution.py:27
  43.1 2.0 pad_maximum_fusion
  45.0 5.1 %copy.32 = f32[3,512,512]{1,0,2:T(4,128)} copy(f32[3,512,512]{2,1,0:T(8,128)} %pad_maximum_fusion) | data formatting | bytes 6291456 | tf_op jit(solution)/shard_map/stack | solution.py:84
  52.0 1.7 fusion.22
  53.8 1.4 fusion.17
  56.1 1.0 fusion.3
  57.2 148.1 %all-reduce.4.cloned.1.call-done = f32[3,512,512]{1,0,2:T(4,128)} async-done(((f32[3,512,512]{1,0,2:T(4,128)}), f32[3,512,512]{1,0,2:T(4,128)}) %all-reduce.4.cloned.1.call-update) | async-done | bytes 3145744
  205.3 1.0 constant_dynamic-slice_fusion
  206.3 7.6 %copy.36 = f32[3,512,32]{0,2,1:T(8,128)} copy(f32[3,512,32]{1,0,2:T(4,128)S(1)} %constant_dynamic-slice_fusion) | data formatting | bytes 393216
  213.9 8.8 %reshape.119 = f32[512,96]{1,0:T(8,128)} reshape(f32[512,32,3]{2,1,0:T(8,128)} %bitcast.108) | data formatting | bytes 393216
  222.8 1.7 convolution_convert_fusion.2
  226.2 5.4 %stack.15 = bf16[8,4,256,512]{3,1,2,0:T(4,128)(2,1)} broadcast(bf16[4,256,512]{2,0,1:T(4,128)(2,1)S(1)} %copy.27), dimensions={1,2,3} | broadcast | bytes 9437184 | tf_op jit(solution)/shard_map/stack | solution.py:98
  231.6 5.4 %all-to-all-start = ((bf16[8,4,256,512]{3,1,2,0:T(4,128)(2,1)}), bf16[8,4,256,512]{3,1,2,0:T(4,128)(2,1)}, u32[]{:S(2)}, u32[]{:S(2)}) async-start(bf16[8,4,256,512]{3,1,2,0:T(4,128)(2,1)} %stack.15), calls=%async_computation | async-start | bytes 16777216 | tf_op jit(solution)/shard_map/all_to_all | solution.py:99
  237.1 1.8 convolution_convert_fusion
  238.9 75.3 %reduce-scatter.4.cloned.1.call-done = f32[64,96]{1,0:T(8,128)} async-done(((f32[512,96]{1,0:T(8,128)}), f32[64,96]{1,0:T(8,128)}) %reduce-scatter.4.cloned.1.call-update) | async-done | bytes 24592
  314.2 1.8 reshape.120
  316.1 1.2 copy.33
  317.3 27.3 %all-to-all-done = bf16[8,4,256,512]{3,1,2,0:T(4,128)(2,1)} async-done(((bf16[8,4,256,512]{3,1,2,0:T(4,128)(2,1)}), bf16[8,4,256,512]{3,1,2,0:T(4,128)(2,1)}, u32[]{:S(2)}, u32[]{:S(2)}) %all-to-all-start) | async-done | bytes 8388640 | tf_op jit(solution)/shard_map/all_to_all | solution.py:99
  344.6 8.6 %copy.28 = bf16[8,4,256,512]{3,1,0,2:T(4,128)(2,1)} copy(bf16[8,4,256,512]{3,1,2,0:T(4,128)(2,1)} %all-to-all-done) | data formatting | bytes 16777216 | tf_op jit(solution)/shard_map/all_to_all | solution.py:99
  353.2 12.5 %reshape.112 = bf16[32,256,512]{2,0,1:T(8,128)(2,1)} reshape(bf16[8,4,256,512]{3,1,0,2:T(4,128)(2,1)} %copy.28) | data formatting | bytes 16777216 | tf_op jit(solution)/shard_map/reshape | solution.py:99
  365.7 6.0 %select_reduce_fusion = (f32[4,256]{0,1:T(8,128)S(1)}, f32[4,32,256]{1,0,2:T(4,128)S(1)}) fusion(pred[4,32]{1,0:T(4,128)(4,1)S(1)} %iota_compare_fusion.2, bf16[32,256,512]{2,0,1:T(8,128)(2,1)} %reshape.112, bf16[4,256,512]{2,1,0:T(8,128)(2,1)} %bitcast.131), kind=kOutput, calls=%fused_computation.64 | convolution fusion | flops 33651712 | bytes 9572480 | tf_op jit(solution)/shard_map/anc,bnc->abn/dot_general | solution.py:102
  372.4 88.8 %all-gather.2.cloned.1.call-done = bf16[32,256,512]{2,1,0:T(8,128)(2,1)} async-done(((bf16[4,256,512]{2,1,0:T(8,128)(2,1)}), bf16[32,256,512]{2,1,0:T(8,128)(2,1)}) %all-gather.2.cloned.1.call-update) | async-done | bytes 8388624 | tf_op jit(solution)/shard_map/all_gather | solution.py:100
  461.2 9.0 %fusion.7 = bf16[4,256,512]{2,0,1:T(4,128)(2,1)S(1)} fusion(bf16[32,256,512]{2,1,0:T(8,128)(2,1)} %all-gather.2.cloned.1.call-done, f32[4,256]{0,1:T(8,128)S(1)} %fusion.56, f32[4,32,256]{1,0,2:T(4,128)S(1)} %get-tuple-element.25, f32[4,256]{0,1:T(8,128)S(1)} %broadcast_maximum_fusion, pred[4,32]{1,0:T(4,128)(4,1)S(1)} %iota_compare_fusion.2), kind=kOutput, calls=%fused_computation.19 | convolution fusion | flops 34668544 | bytes 9576576 | tf_op jit(solution)/shard_map/abn,bnc->anc/dot_general | solution.py:110
  471.2 1.7 fusion.6
  (57 shorter events, 14.2 us)
Async XLA Ops:
  7.2 26.5 %copy-start = (bf16[4,4,64,512]{3,2,1,0:T(8,128)(2,1)S(1)}, bf16[4,4,64,512]{3,2,1,0:T(8,128)(2,1)}, u32[]{:S(2)}) copy-start(bf16[4,4,64,512]{3,2,1,0:T(8,128)(2,1)} %param.17) | copy-start | bytes 3145732
  7.2 198.1 %all-reduce.4.cloned.1.call-start = ((), (), s32[]{:S(2)}) async-start(), calls=%async_computation.4 | async-start | bytes 8388608
  8.4 12.8 %copy-start.2 = (bf16[4,4,64,512]{3,2,1,0:T(8,128)(2,1)S(1)}, bf16[4,4,64,512]{3,2,1,0:T(8,128)(2,1)}, u32[]{:S(2)}) copy-start(bf16[4,4,64,512]{3,2,1,0:T(8,128)(2,1)} %param.9) | copy-start | bytes 3145732
  8.4 9.1 %collective-permute-start = (bf16[4,1,64,512]{3,2,1,0:T(8,128)(2,1)S(1)}, bf16[4,1,64,512]{3,2,1,0:T(8,128)(2,1)S(1)}, u32[]{:S(2)}, u32[]{:S(2)}) collective-permute-start(bf16[4,1,64,512]{3,2,1,0:T(8,128)(2,1)S(1)} %get-tuple-element.20), channel_id=1, source_target_pairs={{0,1},{1,2},{2,3},{3,4},{4,5},{5,6},{6,7},{7,8},{8,9},{9,10},{10,1... | collective-permute-start | bytes 786440 | tf_op jit(solution)/shard_map/ppermute | solution.py:15
  13.5 7.7 %collective-permute-start.1 = (bf16[4,1,64,512]{3,2,1,0:T(8,128)(2,1)S(1)}, bf16[4,1,64,512]{3,2,1,0:T(8,128)(2,1)S(1)}, u32[]{:S(2)}, u32[]{:S(2)}) collective-permute-start(bf16[4,1,64,512]{3,2,1,0:T(8,128)(2,1)S(1)} %get-tuple-element.21), channel_id=1, source_target_pairs={{1,0},{2,1},{3,2},{4,3},{5,4},{6,5},{7,6},{8,7},{9,8},{10,9},{11,1... | collective-permute-start | bytes 786440 | tf_op jit(solution)/shard_map/ppermute | solution.py:17
  21.2 2.3 slice-start
  22.1 1.6 slice-start.1
  30.5 11.0 %collective-permute-start.2 = (bf16[2,4,64,512]{3,2,1,0:T(8,128)(2,1)S(1)}, bf16[2,4,64,512]{3,2,1,0:T(8,128)(2,1)S(1)}, u32[]{:S(2)}, u32[]{:S(2)}) collective-permute-start(bf16[2,4,64,512]{3,2,1,0:T(8,128)(2,1)S(1)} %bitcast.130), channel_id=1, source_target_pairs={{0,16},{16,32},{32,48},{48,64},{64,80},{80,96},{96,112},{1,17},{17... | collective-permute-start | bytes 1572872 | tf_op jit(solution)/shard_map/ppermute | solution.py:27
  41.5 0.8 copy-start.4
  50.2 0.7 copy-start.10
  50.2 264.0 %reduce-scatter.4.cloned.1.call-start = ((), (), s32[]{:S(2)}) async-start(), calls=%async_computation.3 | async-start | bytes 294912
  53.8 1.6 copy-start.3
  213.9 8.9 %copy-start.5 = (bf16[512,512]{1,0:T(8,128)(2,1)S(1)}, bf16[512,512]{1,0:T(8,128)(2,1)}, u32[]{:S(2)}) copy-start(bf16[512,512]{1,0:T(8,128)(2,1)} %param.15) | copy-start | bytes 1572868
  213.9 8.9 %copy-start.9 = (f32[512]{0:T(512)S(1)}, f32[512]{0:T(512)}, u32[]{:S(2)}) copy-start(f32[512]{0:T(512)} %param.12) | copy-start | bytes 6148
  222.7 238.4 %all-gather.2.cloned.1.call-start = ((), (), s32[]{:S(2)}) async-start(), calls=%async_computation.2 | async-start | bytes 9437184 | tf_op jit(solution)/shard_map/all_gather | solution.py:100
  222.8 1.8 copy-start.6
  231.6 5.5 %copy-start.7 = (bf16[512,512]{1,0:T(8,128)(2,1)S(1)}, bf16[512,512]{1,0:T(8,128)(2,1)}, u32[]{:S(2)}) copy-start(bf16[512,512]{1,0:T(8,128)(2,1)} %param.13) | copy-start | bytes 1572868
  231.6 113.0 %all-to-all-start = ((bf16[8,4,256,512]{3,1,2,0:T(4,128)(2,1)}), bf16[8,4,256,512]{3,1,2,0:T(4,128)(2,1)}, u32[]{:S(2)}, u32[]{:S(2)}) async-start(bf16[8,4,256,512]{3,1,2,0:T(4,128)(2,1)} %stack.15), calls=%async_computation | async-start | bytes 16777216 | tf_op jit(solution)/shard_map/all_to_all | solution.py:99
  470.2 1.0 copy-start.8
  470.2 2.7 copy-start.1
Sparse Core Ops, SparseCore 0:
  50.3 154.9 all-reduce.3
  222.8 91.3 reduce-scatter.3
  316.5 144.5 all-gather.1
